TPU v7x, 256 devices: a whole 4x4x8 slice. The times are simulated.
256 devices in a mesh: seq: 64 (over x, z, core), chan: 4 (over y).
Axes of the slice: x: 4, y: 4, z: 8, core: 2. Of those that a mesh axis runs over, the one named last changes fastest.
Arguments:
- signal: bfloat16 [8192, 4096], P('seq', 'chan'), may hold values from -6 to 6
- gate: bfloat16 [8192, 4096], P('seq', 'chan'), may hold values from -6 to 6
- curvature: bfloat16 [8192, 4096], P('seq', 'chan'), may hold values from -6 to 6
- filters: bfloat16 [8192, 8], P('seq'), may hold values from -0.0625 to 0.0625
- probe: int32 [8192, 8], P('seq'), may hold values from 0 to 1
- group_ids: int32 [4096], P('chan'), may hold values from 0 to 7
Outputs:
- gated_output: bfloat16 [8192, 4096], P('seq', 'chan')
- curvature_probe: bfloat16 [8192, 8], P('seq', 'chan')
Inputs may be any that keep to these rules, and one draw needn't show every extreme that they name: The probe's sign at a tap is 2 * bit - 1.
All inputs are finite; a program needn't handle non-finite values.
Results may differ from a plain program's by a relative error of at most 0.014.
Values may be sent and summed in bfloat16 or wider, within the bound.
A program may use at most 64 MiB of HBM per device.

v0:
```python
import functools
import math

import jax
import jax.numpy as jnp
import numpy as np
from jax import lax
from jax.experimental import pallas as pl
from jax.experimental.pallas import tpu as pltpu
from jax.sharding import PartitionSpec as P

SPAN = 128
HALF = 64
KEPT = 80
BF16 = jnp.bfloat16
F32 = jnp.float32


def tables():
    total = SPAN * SPAN
    k2 = np.arange(KEPT)
    live = (k2 <= SPAN // 2).astype(np.float64)
    n1 = np.arange(HALF)
    outer = 2 * np.pi * (np.outer(k2, n1) % SPAN) / SPAN
    enter = np.concatenate([np.cos(outer) * live[:, None], -np.sin(outer) * live[:, None]])
    weight = live * np.where((k2 == 0) | (k2 == SPAN // 2), 1.0, 2.0)
    leave = np.concatenate([(np.cos(outer) * weight[:, None]).T, (-np.sin(outer) * weight[:, None]).T], axis=1)
    fine = np.arange(SPAN)
    twist = 2 * np.pi * np.outer(k2, fine) / total
    turn = np.concatenate([np.cos(twist), np.sin(twist)], axis=1)
    inner = 2 * np.pi * (np.outer(fine, fine) % SPAN) / SPAN
    cos, sin = np.cos(inner), np.sin(inner)
    ahead = np.block([[cos, -sin], [sin, cos]])
    back = np.block([[cos, sin], [-sin, cos]])
    cast = lambda a: a.astype(np.float32).astype(BF16)
    return cast(enter), cast(leave), turn.astype(np.float32), cast(ahead), cast(back)


def dot(a, b):
    return jnp.dot(a, b, preferred_element_type=F32)


def spread_columns(src, wide, cols):
    width = src.shape[1]
    wide[...] = src[...].astype(F32).reshape(HALF * width, SPAN)
    for c in range(width):
        cols[:, c * SPAN : (c + 1) * SPAN] = wide[pl.ds(c, HALF, stride=width), :].astype(BF16)


def forward(cols, enter, turn, ahead, rows, spec):
    width = spec.shape[0]
    tc, ts = turn[:, :SPAN], turn[:, SPAN:]
    for q in range(0, width, 4):
        mixed = dot(enter[...], cols[:, q * SPAN : (q + 4) * SPAN])
        for c in range(4):
            re = mixed[:KEPT, c * SPAN : (c + 1) * SPAN]
            im = mixed[KEPT:, c * SPAN : (c + 1) * SPAN]
            r0 = (q + c) * KEPT
            rows[r0 : r0 + KEPT, :SPAN] = (re * tc + im * ts).astype(BF16)
            rows[r0 : r0 + KEPT, SPAN:] = (im * tc - re * ts).astype(BF16)
    for q in range(0, width, 4):
        spec[q : q + 4] = dot(rows[q * KEPT : (q + 4) * KEPT, :], ahead[...]).reshape(4, KEPT, 2 * SPAN)


def untwist(block, tc, ts):
    re, im = block[:, :SPAN], block[:, SPAN:]
    return jnp.concatenate([re * tc - im * ts, im * tc + re * ts], axis=0).astype(BF16)


def transform_body(sig, taps, mix, gid, enter, leave, turn, ahead, back, prim, part,
                   wide, cols, rows, sig_spec, tap_spec, back_spec, group_spec):
    width = sig.shape[1]
    groups = tap_spec.shape[0] // 2
    total = SPAN * SPAN
    probe_scale = 1.0 / math.sqrt(HALF * SPAN)
    tc, ts = turn[:, :SPAN], turn[:, SPAN:]
    spread_columns(sig, wide, cols)
    forward(cols, enter, turn, ahead, rows, sig_spec)
    spread_columns(taps, wide, cols)
    forward(cols, enter, turn, ahead, rows, tap_spec)
    wide[...] = mix[...].astype(F32).reshape(HALF * width, SPAN)
    for c in range(width):
        g = gid[c]
        sr, si = sig_spec[c, :, :SPAN], sig_spec[c, :, SPAN:]
        for kind in range(2):
            fr, fi = tap_spec[g + kind * groups, :, :SPAN], tap_spec[g + kind * groups, :, SPAN:]
            r0 = kind * KEPT
            rows[r0 : r0 + KEPT, :SPAN] = (sr * fr - si * fi).astype(BF16)
            rows[r0 : r0 + KEPT, SPAN:] = (sr * fi + si * fr).astype(BF16)
        inner = dot(rows[: 2 * KEPT, :], back[...])
        both = jnp.concatenate([untwist(inner[:KEPT], tc, ts), untwist(inner[KEPT:], tc, ts)], axis=1)
        timed = dot(leave[...], both)
        weight = wide[pl.ds(c, HALF, stride=width), :]
        wide[pl.ds(c, HALF, stride=width), :] = timed[:, :SPAN] * (1.0 / total)
        tangent = (timed[:, SPAN:] * (probe_scale / total)).astype(BF16).astype(F32)
        cols[:, c * SPAN : (c + 1) * SPAN] = (tangent * weight).astype(BF16)
    prim[...] = wide[...].astype(BF16).reshape(prim.shape)
    forward(cols, enter, turn, ahead, rows, back_spec)
    for c in range(width):
        sr, si = sig_spec[c, :, :SPAN], sig_spec[c, :, SPAN:]
        br, bi = back_spec[c, :, :SPAN], back_spec[c, :, SPAN:]
        back_spec[c] = jnp.concatenate([sr * br + si * bi, sr * bi - si * br], axis=1)
    for g in range(groups):
        acc = jnp.zeros((KEPT, 2 * SPAN), F32)
        for c in range(width):
            acc = acc + jnp.where(gid[c] == g, 1.0, 0.0).astype(F32) * back_spec[c]
        group_spec[g * KEPT : (g + 1) * KEPT, :] = acc.astype(BF16)
    for g in range(0, groups, 2):
        inner = dot(group_spec[g * KEPT : (g + 2) * KEPT, :], back[...])
        both = jnp.concatenate([untwist(inner[:KEPT], tc, ts), untwist(inner[KEPT:], tc, ts)], axis=1)
        timed = dot(leave[...], both)
        part[g] = timed[:, :SPAN]
        part[g + 1] = timed[:, SPAN:]


def transform(sig, taps, mix, gid, groups):
    width = sig.shape[1]
    vmem = pl.BlockSpec(memory_space=pltpu.VMEM)
    return pl.pallas_call(
        transform_body,
        out_shape=(
            jax.ShapeDtypeStruct(sig.shape, BF16),
            jax.ShapeDtypeStruct((groups, HALF, SPAN), F32),
        ),
        in_specs=[vmem] * 3 + [pl.BlockSpec(memory_space=pltpu.SMEM)] + [vmem] * 5,
        out_specs=(vmem, vmem),
        scratch_shapes=[
            pltpu.VMEM((HALF * width, SPAN), F32),
            pltpu.VMEM((HALF, width * SPAN), BF16),
            pltpu.VMEM((width * KEPT, 2 * SPAN), BF16),
            pltpu.VMEM((width, KEPT, 2 * SPAN), F32),
            pltpu.VMEM((2 * groups, KEPT, 2 * SPAN), F32),
            pltpu.VMEM((width, KEPT, 2 * SPAN), F32),
            pltpu.VMEM((groups * KEPT, 2 * SPAN), BF16),
        ],
        compiler_params=pltpu.CompilerParams(vmem_limit_bytes=40 << 20),
    )(sig, taps, mix, gid, *[jnp.asarray(t) for t in tables()])


def local(signal, gate, curvature, filters, probe, group_ids):
    devices = lax.axis_size("seq")
    position = lax.axis_index("seq")
    seq_rows, chan_width = signal.shape
    groups = filters.shape[1]
    width = chan_width // devices
    gate_float = gate.astype(F32)
    mix = (gate_float * gate_float * curvature.astype(F32)).astype(BF16)
    taps = jnp.concatenate([filters, (2 * probe - 1).astype(BF16)], axis=1).T
    tiled = lambda a: a.T.reshape(devices, width, seq_rows)
    sent = jnp.stack([tiled(signal), jnp.broadcast_to(taps[None], (devices, width, seq_rows)), tiled(mix)], axis=1)
    got = lax.all_to_all(sent, "seq", split_axis=0, concat_axis=0, tiled=True)
    own = lax.dynamic_slice_in_dim(group_ids, position * width, width, 0)
    prim, part = transform(got[:, 0], got[:, 1], got[:, 2], own, groups)
    home = lax.all_to_all(prim, "seq", split_axis=0, concat_axis=0, tiled=True)
    output_mix = (gate_float * home.reshape(chan_width, seq_rows).T.astype(F32)).astype(BF16)
    summed = lax.psum_scatter(part, "chan", scatter_dimension=0, tiled=True)
    summed = lax.psum_scatter(summed, "seq", scatter_dimension=1, tiled=True)
    length = seq_rows * devices
    total_width = chan_width * lax.axis_size("chan")
    scale = 1.0 / (math.sqrt(length * total_width / groups) * SPAN * SPAN)
    return (output_mix, (summed[:, 0, :].T * scale).astype(BF16))


def solution(mesh):
    return jax.shard_map(
        local,
        mesh=mesh,
        in_specs=(
            P("seq", "chan"),
            P("seq", "chan"),
            P("seq", "chan"),
            P("seq", None),
            P("seq", None),
            P("chan"),
        ),
        out_specs=(P("seq", "chan"), P("seq", "chan")),
        check_vma=False,
    )
```

profile of v0, /device:TPU:1, one launch (start us, length us, event | category | flops | bytes accessed | tf_op | source)
XLA Modules:
  0.0 272.3 jit_solution(13568842962925995688)
XLA Ops:
  7.2 1.1 fusion.3
  8.3 0.2 copy.20
  8.5 0.5 copy-done.7
  9.0 0.3 copy-done.6
  9.3 0.2 copy.19
  9.4 0.5 copy-done.8
  10.0 1.0 pad_maximum_fusion
  11.0 13.0 %all-to-all-start = ((bf16[64,3,16,128]{3,2,1,0:T(8,128)(2,1)}), bf16[64,3,16,128]{3,2,1,0:T(8,128)(2,1)S(1)}, u32[]{:S(2)}, u32[]{:S(2)}) async-start(bf16[64,3,16,128]{3,2,1,0:T(8,128)(2,1)} %pad_maximum_fusion), calls=%async_computation | async-start | bytes 1572864 | tf_op jit(solution)/shard_map/all_to_all | solution.py:151
  23.9 0.8 dynamic_slice.3.gid
  24.7 22.1 %all-to-all-done = bf16[64,3,16,128]{3,2,1,0:T(8,128)(2,1)S(1)} async-done(((bf16[64,3,16,128]{3,2,1,0:T(8,128)(2,1)}), bf16[64,3,16,128]{3,2,1,0:T(8,128)(2,1)S(1)}, u32[]{:S(2)}, u32[]{:S(2)}) %all-to-all-start) | async-done | bytes 786464 | tf_op jit(solution)/shard_map/all_to_all | solution.py:151
  46.9 0.1 slice_bitcast_fusion
  47.1 8.4 %shard_map.122 = (bf16[64,16,128]{2,1,0:T(8,128)(2,1)}, f32[8,64,128]{2,1,0:T(8,128)}) custom-call(bf16[64,16,128]{2,1,0:T(8,128)(2,1)S(1)} %get-tuple-element.8.sig, bf16[64,16,128]{2,1,0:T(8,128)(2,1)S(1)} %get-tuple-element.7.taps, bf16[64,16,128]{2,1,0:T(8,128)(2,1)S(1)} %get-tuple-element.6.mix, s32[16]{0:T(128)S(1)} %dynamic_slice.3.gid, ...), custom_call_target="tpu_custom_call" | custom-call | tf_op jit(solution)/shard_map/pallas_call | solution.py:119
  55.4 6.2 %all-to-all-start.1 = ((bf16[64,16,128]{2,1,0:T(8,128)(2,1)}), bf16[64,16,128]{2,1,0:T(8,128)(2,1)S(1)}, u32[]{:S(2)}, u32[]{:S(2)}) async-start(bf16[64,16,128]{2,1,0:T(8,128)(2,1)} %get-tuple-element.4), calls=%async_computation.1 | async-start | bytes 524288 | tf_op jit(solution)/shard_map/all_to_all | solution.py:154
  61.7 0.7 reduce-scatter.2.cloned.1.call-update
  62.4 0.7 copy-done.9
  63.1 0.6 dynamic-slice
  63.8 9.8 %all-to-all-done.1 = bf16[64,16,128]{2,1,0:T(8,128)(2,1)S(1)} async-done(((bf16[64,16,128]{2,1,0:T(8,128)(2,1)}), bf16[64,16,128]{2,1,0:T(8,128)(2,1)S(1)}, u32[]{:S(2)}, u32[]{:S(2)}) %all-to-all-start.1) | async-done | bytes 262176 | tf_op jit(solution)/shard_map/all_to_all | solution.py:154
  73.6 0.1 bitcast_convert_fusion
  73.7 0.2 copy.24
  73.9 13.4 %reduce-scatter.2.cloned.1.call-done = f32[2,64,128]{2,1,0:T(8,128)} async-done(((f32[8,64,128]{2,1,0:T(8,128)}), f32[2,64,128]{2,1,0:T(8,128)}) %reduce-scatter.2.cloned.1.call-update) | async-done | bytes 65552 | tf_op jit(solution)/shard_map/reduce_scatter | solution.py:156
  87.3 1.5 copy.25
  88.8 0.8 fusion.2
  89.6 174.0 %all-reduce.3.cloned.1.call-done = f32[2,64,128]{2,0,1:T(2,128)} async-done(((f32[2,64,128]{2,0,1:T(2,128)}), f32[2,64,128]{2,0,1:T(2,128)}) %all-reduce.3.cloned.1.call-update) | async-done | bytes 65552
  263.6 1.8 fusion.5
  (22 shorter events, 0.2 us)
Async XLA Ops:
  8.3 0.7 copy-start.7
  8.3 1.0 copy-start.6
  9.2 0.7 copy-start.8
  11.0 35.9 %all-to-all-start = ((bf16[64,3,16,128]{3,2,1,0:T(8,128)(2,1)}), bf16[64,3,16,128]{3,2,1,0:T(8,128)(2,1)S(1)}, u32[]{:S(2)}, u32[]{:S(2)}) async-start(bf16[64,3,16,128]{3,2,1,0:T(8,128)(2,1)} %pad_maximum_fusion), calls=%async_computation | async-start | bytes 1572864 | tf_op jit(solution)/shard_map/all_to_all | solution.py:151
  24.7 22.3 %copy-start = (bf16[256,256]{1,0:T(8,128)(2,1)S(1)}, bf16[256,256]{1,0:T(8,128)(2,1)}, u32[]{:S(2)}) copy-start(bf16[256,256]{1,0:T(8,128)(2,1)} %constant.32.clone.ahead) | copy-start | bytes 393220
  24.7 22.3 %copy-start.1 = (bf16[256,256]{1,0:T(8,128)(2,1)S(1)}, bf16[256,256]{1,0:T(8,128)(2,1)}, u32[]{:S(2)}) copy-start(bf16[256,256]{1,0:T(8,128)(2,1)} %constant.33.clone.back) | copy-start | bytes 393220
  24.7 22.3 %copy-start.2 = (f32[80,256]{1,0:T(8,128)S(1)}, f32[80,256]{1,0:T(8,128)}, u32[]{:S(2)}) copy-start(f32[80,256]{1,0:T(8,128)} %constant.31.clone.turn) | copy-start | bytes 245764
  24.7 22.3 %copy-start.3 = (bf16[160,64]{1,0:T(8,128)(2,1)S(1)}, bf16[160,64]{1,0:T(8,128)(2,1)}, u32[]{:S(2)}) copy-start(bf16[160,64]{1,0:T(8,128)(2,1)} %constant.29.clone.enter) | copy-start | bytes 61444
  24.7 22.3 %copy-start.4 = (bf16[64,160]{1,0:T(8,128)(2,1)S(1)}, bf16[64,160]{1,0:T(8,128)(2,1)}, u32[]{:S(2)}) copy-start(bf16[64,160]{1,0:T(8,128)(2,1)} %constant.30.clone.leave) | copy-start | bytes 61444
  55.4 18.2 %all-to-all-start.1 = ((bf16[64,16,128]{2,1,0:T(8,128)(2,1)}), bf16[64,16,128]{2,1,0:T(8,128)(2,1)S(1)}, u32[]{:S(2)}, u32[]{:S(2)}) async-start(bf16[64,16,128]{2,1,0:T(8,128)(2,1)} %get-tuple-element.4), calls=%async_computation.1 | async-start | bytes 524288 | tf_op jit(solution)/shard_map/all_to_all | solution.py:154
  61.6 25.6 %reduce-scatter.2.cloned.1.call-start = ((), (), s32[]{:S(2)}) async-start(), calls=%async_computation.3 | async-start | bytes 327680 | tf_op jit(solution)/shard_map/reduce_scatter | solution.py:156
  62.4 201.2 %all-reduce.3.cloned.1.call-start = ((), (), s32[]{:S(2)}) async-start(), calls=%async_computation.4 | async-start | bytes 131072
  62.4 0.7 copy-start.9
  73.7 15.1 %copy-start.5 = (bf16[128,1024]{1,0:T(8,128)(2,1)S(1)}, bf16[128,1024]{1,0:T(8,128)(2,1)}, u32[]{:S(2)}) copy-start(bf16[128,1024]{1,0:T(8,128)(2,1)} %param.12) | copy-start | bytes 786436
Sparse Core Ops, SparseCore 0:
  65.0 22.2 reduce-scatter.1
  90.7 172.8 all-reduce.2
where the time goes:
time: 273 us; the launch traced here: 272 us
  waiting for transfers between devices  220 us (81%)
  starting transfers between devices  19.3 us (7%)
  between operations  14.2 us (5%)
  Pallas kernels  8.36 us (3%)
  local copies, waits for them, and re-layouts  5.6 us (2%)
  other arithmetic  4.76 us (2%)
    unnamed x3, waiting for transfers between devices  175 us
    all_to_all x1, waiting for transfers between devices, local(): got = lax.all_to_all(sent, 'seq', split_axis=0, concat_axis=0, tiled=True)  22.1 us
    reduce_scatter x1, waiting for transfers between devices, local(): summed = lax.psum_scatter(part, 'chan', scatter_dimension=0, tiled=True)  13.4 us
    all_to_all x1, starting transfers between devices, local(): got = lax.all_to_all(sent, 'seq', split_axis=0, concat_axis=0, tiled=True)  13 us
    all_to_all x1, waiting for transfers between devices, local(): home = lax.all_to_all(prim, 'seq', split_axis=0, concat_axis=0, tiled=True)  9.85 us
    pallas_call x1, Pallas kernels, transform(): pl.pallas_call(transform_body, out_shape=(jax.ShapeDtypeStruct(sig.shape,...  8.36 us
    all_to_all x1, starting transfers between devices, local(): home = lax.all_to_all(prim, 'seq', split_axis=0, concat_axis=0, tiled=True)  6.22 us
  transfers between devices with their start and end apart: 4, of which 4 were waited for; matrix products, arithmetic and copies ran while one was open for 1% of the time, Pallas kernels for 0%

commit v1 on v0

v1 whole, which is shorter than its diff:
```python
import math

import jax
import jax.numpy as jnp
import numpy as np
from jax import lax
from jax.experimental import pallas as pl
from jax.experimental.pallas import tpu as pltpu
from jax.sharding import PartitionSpec as P

SPAN = 128
HALF = 64
KEPT = 80
BF16 = jnp.bfloat16
F32 = jnp.float32
MESH = pl.DeviceIdType.MESH


def tables():
    total = SPAN * SPAN
    k2 = np.arange(KEPT)
    live = (k2 <= SPAN // 2).astype(np.float64)
    n1 = np.arange(HALF)
    outer = 2 * np.pi * (np.outer(k2, n1) % SPAN) / SPAN
    enter = np.concatenate([np.cos(outer) * live[:, None], -np.sin(outer) * live[:, None]])
    weight = live * np.where((k2 == 0) | (k2 == SPAN // 2), 1.0, 2.0)
    leave = np.concatenate([(np.cos(outer) * weight[:, None]).T, (-np.sin(outer) * weight[:, None]).T], axis=1)
    fine = np.arange(SPAN)
    twist = 2 * np.pi * np.outer(k2, fine) / total
    turn = np.concatenate([np.cos(twist), np.sin(twist)], axis=1)
    inner = 2 * np.pi * (np.outer(fine, fine) % SPAN) / SPAN
    cos, sin = np.cos(inner), np.sin(inner)
    ahead = np.block([[cos, -sin], [sin, cos]])
    back = np.block([[cos, sin], [-sin, cos]])
    cast = lambda a: a.astype(np.float32).astype(BF16)
    return cast(enter), cast(leave), turn.astype(np.float32), cast(ahead), cast(back)


def dot(a, b):
    return jnp.dot(a, b, preferred_element_type=F32)


def spread_columns(src, wide, cols):
    width = src.shape[1]
    wide[...] = src[...].astype(F32).reshape(HALF * width, SPAN)
    for c in range(width):
        cols[:, c * SPAN : (c + 1) * SPAN] = wide[pl.ds(c, HALF, stride=width), :].astype(BF16)


def forward(cols, enter, turn, ahead, rows, spec):
    width = spec.shape[0]
    tc, ts = turn[:, :SPAN], turn[:, SPAN:]
    for q in range(0, width, 4):
        mixed = dot(enter[...], cols[:, q * SPAN : (q + 4) * SPAN])
        for c in range(4):
            re = mixed[:KEPT, c * SPAN : (c + 1) * SPAN]
            im = mixed[KEPT:, c * SPAN : (c + 1) * SPAN]
            r0 = (q + c) * KEPT
            rows[r0 : r0 + KEPT, :SPAN] = (re * tc + im * ts).astype(BF16)
            rows[r0 : r0 + KEPT, SPAN:] = (im * tc - re * ts).astype(BF16)
    for q in range(0, width, 4):
        spec[q : q + 4] = dot(rows[q * KEPT : (q + 4) * KEPT, :], ahead[...]).reshape(4, KEPT, 2 * SPAN)


def untwist(block, tc, ts):
    re, im = block[:, :SPAN], block[:, SPAN:]
    return jnp.concatenate([re * tc - im * ts, im * tc + re * ts], axis=0).astype(BF16)


def tiles_of(block):
    return block.astype(F32).T.astype(BF16)


def body(signal, gate, curvature, filters, probe, gid, enter, leave, turn, ahead, back, gated, curved,
         sig_out, sig_in, tap_out, tap_in, mix_out, mix_in, prim_out, home, part_out, part_in, sum_out, sum_in,
         wide, cols, rows, sig_spec, tap_spec, back_spec, group_spec, send, recv):
    me = lax.axis_index("seq")
    lane = lax.axis_index("chan")
    peers = lax.axis_size("seq")
    lanes = lax.axis_size("chan")
    width = sig_in.shape[1]
    chans = width * peers
    groups = filters.shape[0]
    total = SPAN * SPAN
    probe_scale = 1.0 / math.sqrt(HALF * SPAN)
    tc, ts = turn[:, :SPAN], turn[:, SPAN:]

    barrier = pltpu.get_barrier_semaphore()

    @pl.loop(1, peers)
    def _(k):
        pl.semaphore_signal(barrier, inc=1, device_id={"seq": lax.rem(me + k, peers)}, device_id_type=MESH)

    for k in range(1, lanes):
        pl.semaphore_signal(barrier, inc=1, device_id={"chan": lax.rem(lane + k, lanes)}, device_id_type=MESH)

    per = SPAN // width
    for b in range(chans // SPAN):
        sig_out[b * per : (b + 1) * per] = tiles_of(signal[:, b * SPAN : (b + 1) * SPAN]).reshape(per, width, SPAN)
    signs = 2.0 * probe[...].astype(F32) - 1.0
    tap_out[...] = jnp.concatenate([filters[...].astype(F32), signs], axis=0).astype(BF16)
    sig_in[me] = sig_out[me]
    tap_in[me] = tap_out[...]
    pl.semaphore_wait(barrier, peers + lanes - 2)

    def tile_copy(slot, src, dst, to):
        return pltpu.make_async_remote_copy(
            src_ref=src, dst_ref=dst, send_sem=send.at[slot], recv_sem=recv.at[slot],
            device_id={"seq": to}, device_id_type=MESH,
        )

    def scatter(slot, out, into):
        @pl.loop(1, peers)
        def _(k):
            to = lax.rem(me + k, peers)
            tile_copy(slot, out.at[to], into.at[me], to).start()

    def whole(slot, out, into):
        rest = pl.ds(0, peers - 1)
        return tile_copy(slot, out.at[rest], into.at[rest], lax.rem(me + 1, peers))

    scatter(0, sig_out, sig_in)

    @pl.loop(1, peers)
    def _(k):
        to = lax.rem(me + k, peers)
        tile_copy(1, tap_out, tap_in.at[me], to).start()

    for b in range(chans // SPAN):
        g32 = gate[:, b * SPAN : (b + 1) * SPAN].astype(F32)
        mixed = g32 * g32 * curvature[:, b * SPAN : (b + 1) * SPAN].astype(F32)
        mix_out[b * per : (b + 1) * per] = tiles_of(mixed).reshape(per, width, SPAN)
    mix_in[me] = mix_out[me]
    scatter(2, mix_out, mix_in)

    whole(0, sig_out, sig_in).wait_recv()
    spread_columns(sig_in, wide, cols)
    forward(cols, enter, turn, ahead, rows, sig_spec)
    whole(1, mix_out, tap_in).wait_recv()
    spread_columns(tap_in, wide, cols)
    forward(cols, enter, turn, ahead, rows, tap_spec)
    whole(2, mix_out, mix_in).wait_recv()
    wide[...] = mix_in[...].astype(F32).reshape(HALF * width, SPAN)
    for c in range(width):
        g = gid[me * width + c]
        sr, si = sig_spec[c, :, :SPAN], sig_spec[c, :, SPAN:]
        for kind in range(2):
            taps = tap_spec[g + kind * groups]
            fr, fi = taps[:, :SPAN], taps[:, SPAN:]
            r0 = (2 * c + kind) * KEPT
            rows[r0 : r0 + KEPT, :SPAN] = (sr * fr - si * fi).astype(BF16)
            rows[r0 : r0 + KEPT, SPAN:] = (sr * fi + si * fr).astype(BF16)
        inner = dot(rows[2 * c * KEPT : 2 * (c + 1) * KEPT, :], back[...])
        both = jnp.concatenate([untwist(inner[:KEPT], tc, ts), untwist(inner[KEPT:], tc, ts)], axis=1)
        timed = dot(leave[...], both)
        weight = wide[pl.ds(c, HALF, stride=width), :]
        wide[pl.ds(c, HALF, stride=width), :] = timed[:, :SPAN] * (1.0 / total)
        tangent = (timed[:, SPAN:] * (probe_scale / total)).astype(BF16).astype(F32)
        cols[:, c * SPAN : (c + 1) * SPAN] = (tangent * weight).astype(BF16)
    prim_out[...] = wide[...].astype(BF16).reshape(prim_out.shape)
    home[me] = prim_out[me]
    scatter(3, prim_out, home)

    forward(cols, enter, turn, ahead, rows, back_spec)
    for c in range(width):
        sr, si = sig_spec[c, :, :SPAN], sig_spec[c, :, SPAN:]
        br, bi = back_spec[c, :, :SPAN], back_spec[c, :, SPAN:]
        back_spec[c] = jnp.concatenate([sr * br + si * bi, sr * bi - si * br], axis=1)
    for g in range(groups):
        acc = jnp.zeros((KEPT, 2 * SPAN), F32)
        for c in range(width):
            acc = acc + jnp.where(gid[me * width + c] == g, 1.0, 0.0).astype(F32) * back_spec[c]
        group_spec[g * KEPT : (g + 1) * KEPT, :] = acc.astype(BF16)
    for g in range(0, groups, 2):
        inner = dot(group_spec[g * KEPT : (g + 2) * KEPT, :], back[...])
        both = jnp.concatenate([untwist(inner[:KEPT], tc, ts), untwist(inner[KEPT:], tc, ts)], axis=1)
        timed = dot(leave[...], both)
        wide[pl.ds(g, HALF, stride=groups), :] = timed[:, :SPAN]
        wide[pl.ds(g + 1, HALF, stride=groups), :] = timed[:, SPAN:]
    part_out[...] = wide[: HALF * groups, :].reshape(part_out.shape)
    part_in[me] = part_out[me]
    scatter(4, part_out, part_in)

    whole(3, prim_out, home).wait_recv()
    for b in range(chans // SPAN):
        block = home[b * per : (b + 1) * per].reshape(SPAN, SPAN)
        lot = slice(b * SPAN, (b + 1) * SPAN)
        gated[:, lot] = (gate[:, lot].astype(F32) * block.astype(F32).T).astype(BF16)

    whole(4, part_out, part_in).wait_recv()
    sum_out[...] = jnp.sum(part_in[...], axis=0)
    sum_in[lane] = sum_out[...]
    gathers = []
    for k in range(1, lanes):
        to = lax.rem(lane + k, lanes)
        copy = pltpu.make_async_remote_copy(
            src_ref=sum_out, dst_ref=sum_in.at[lane], send_sem=send.at[4 + k], recv_sem=recv.at[4 + k],
            device_id={"chan": to}, device_id_type=MESH,
        )
        copy.start()
        gathers.append(copy)
    whole(0, sig_out, sig_in).wait_send()
    whole(1, sig_out, sig_in).wait_send()
    whole(2, mix_out, mix_in).wait_send()
    whole(3, prim_out, home).wait_send()
    whole(4, part_out, part_in).wait_send()
    for copy in gathers:
        copy.wait()
    scale = 1.0 / (math.sqrt(HALF * SPAN * chans * lanes / groups) * total)
    curved[...] = jnp.sum(sum_in[...], axis=0) * scale


def local(signal, gate, curvature, filters, probe, group_ids):
    peers, lanes = lax.axis_size("seq"), lax.axis_size("chan")
    seq_rows, chans = signal.shape
    groups = filters.shape[1]
    width = chans // peers
    vmem = pl.BlockSpec(memory_space=pltpu.VMEM)
    tile = pltpu.VMEM((peers, width, seq_rows), BF16)
    output_mix, curved = pl.pallas_call(
        body,
        out_shape=(
            jax.ShapeDtypeStruct((seq_rows, chans), BF16),
            jax.ShapeDtypeStruct((groups, seq_rows), F32),
        ),
        in_specs=[vmem] * 5 + [pl.BlockSpec(memory_space=pltpu.SMEM)] + [vmem] * 5,
        out_specs=(vmem, vmem),
        scratch_shapes=[
            tile,
            tile,
            pltpu.VMEM((width, seq_rows), BF16),
            tile,
            tile,
            tile,
            tile,
            tile,
            pltpu.VMEM((peers, groups, seq_rows), F32),
            pltpu.VMEM((peers, groups, seq_rows), F32),
            pltpu.VMEM((groups, seq_rows), F32),
            pltpu.VMEM((lanes, groups, seq_rows), F32),
            pltpu.VMEM((HALF * width, SPAN), F32),
            pltpu.VMEM((HALF, width * SPAN), BF16),
            pltpu.VMEM((2 * width * KEPT, 2 * SPAN), BF16),
            pltpu.VMEM((width, KEPT, 2 * SPAN), F32),
            pltpu.VMEM((2 * groups, KEPT, 2 * SPAN), F32),
            pltpu.VMEM((width, KEPT, 2 * SPAN), F32),
            pltpu.VMEM((groups * KEPT, 2 * SPAN), BF16),
            pltpu.SemaphoreType.DMA((4 + lanes,)),
            pltpu.SemaphoreType.DMA((4 + lanes,)),
        ],
        compiler_params=pltpu.CompilerParams(
            collective_id=0, has_side_effects=True, vmem_limit_bytes=40 << 20
        ),
    )(signal, gate, curvature, filters.T, probe.T, group_ids, *[jnp.asarray(t) for t in tables()])
    share = groups // lanes
    mine = lax.dynamic_slice_in_dim(curved, lax.axis_index("chan") * share, share, 0)
    return (output_mix, mine.T.astype(BF16))


def solution(mesh):
    return jax.shard_map(
        local,
        mesh=mesh,
        in_specs=(
            P("seq", "chan"),
            P("seq", "chan"),
            P("seq", "chan"),
            P("seq", None),
            P("seq", None),
            P("chan"),
        ),
        out_specs=(P("seq", "chan"), P("seq", "chan")),
        check_vma=False,
    )
```

time: 273 us -> 64.3 us (0.24)
  waiting for transfers between devices: 220 us -> 0 us
  Pallas kernels: 8.36 us -> 54.2 us
  starting transfers between devices: 19.3 us -> 0 us
  between operations: 14.2 us -> 0.68 us
  other arithmetic: 4.76 us -> 0 us
  local copies, waits for them, and re-layouts: 5.6 us -> 9 us
    unnamed x3 -> x0, waiting for transfers between devices: 175 us -> none
    pallas_call x1, Pallas kernels: 8.36 us -> 54.2 us  [local(): pl.pallas_call(body, out_shape=(jax.ShapeDtypeStruct((seq_rows, chans), B...]
    all_to_all x2 -> x0, waiting for transfers between devices: 32 us -> none  [the longest x1 22.1 us: local(): got = lax.all_to_all(sent, 'seq', split_axis=0, concat_axis=0, tiled=True)]
    all_to_all x2 -> x0, starting transfers between devices: 19.2 us -> none  [the longest x1 13 us: local(): got = lax.all_to_all(sent, 'seq', split_axis=0, concat_axis=0, tiled=True)]
    reduce_scatter x1 -> x0, waiting for transfers between devices: 13.4 us -> none  [local(): summed = lax.psum_scatter(part, 'chan', scatter_dimension=0, tiled=True)]
    unnamed x21 -> x23, local copies, waits for them, and re-layouts: 2.63 us -> 8.47 us
  transfers between devices with their start and end apart: 4 -> 0, of which waited for: 4 -> 0; matrix products, arithmetic and copies ran while one was open for 1% -> 0% of each run, Pallas kernels for 0% -> 0%
where the time goes in v1:
time: 64.3 us; the launch traced here: 63.9 us
  Pallas kernels  54.2 us (84%)
  local copies, waits for them, and re-layouts  9 us (14%)
  between operations  0.68 us (1%)
    pallas_call x1, Pallas kernels, local(): pl.pallas_call(body, out_shape=(jax.ShapeDtypeStruct((seq_rows, chans), B...  54.2 us
    unnamed x23, local copies, waits for them, and re-layouts  8.47 us

profile of v1, /device:TPU:1, one launch (start us, length us, event | category | flops | bytes accessed | tf_op | source)
XLA Modules:
  0.0 63.9 jit_solution(214699837373913711)
XLA Ops:
  0.6 0.0 copy-start.10
  0.6 0.0 copy-start.9
  0.7 0.0 copy-start.8
  0.7 0.7 %copy-done.10 = bf16[128,8]{0,1:T(8,128)(2,1)S(1)} copy-done((bf16[128,8]{0,1:T(8,128)(2,1)S(1)}, bf16[128,8]{0,1:T(8,128)(2,1)}, u32[]{:S(2)}) %copy-start.10) | copy-done | bytes 2072
  1.3 0.0 copy-done.9
  1.3 0.0 copy-done.8
  1.4 0.0 copy-start
  1.4 0.9 %copy-done = bf16[128,1024]{1,0:T(8,128)(2,1)S(1)} copy-done((bf16[128,1024]{1,0:T(8,128)(2,1)S(1)}, bf16[128,1024]{1,0:T(8,128)(2,1)}, u32[]{:S(2)}) %copy-start) | copy-done | bytes 262168
  2.3 0.0 copy-start.1
  2.3 0.9 %copy-done.1 = bf16[128,1024]{1,0:T(8,128)(2,1)S(1)} copy-done((bf16[128,1024]{1,0:T(8,128)(2,1)S(1)}, bf16[128,1024]{1,0:T(8,128)(2,1)}, u32[]{:S(2)}) %copy-start.1) | copy-done | bytes 262168
  3.3 0.0 copy-start.2
  3.3 0.9 %copy-done.2 = bf16[128,1024]{1,0:T(8,128)(2,1)S(1)} copy-done((bf16[128,1024]{1,0:T(8,128)(2,1)S(1)}, bf16[128,1024]{1,0:T(8,128)(2,1)}, u32[]{:S(2)}) %copy-start.2) | copy-done | bytes 262168
  4.2 0.9 %copy-done.3 = bf16[256,256]{1,0:T(8,128)(2,1)S(1)} copy-done((bf16[256,256]{1,0:T(8,128)(2,1)S(1)}, bf16[256,256]{1,0:T(8,128)(2,1)}, u32[]{:S(2)}) %copy-start.3) | copy-done | bytes 131096
  5.1 0.0 copy-start.4
  5.1 0.9 %copy-done.4 = bf16[256,256]{1,0:T(8,128)(2,1)S(1)} copy-done((bf16[256,256]{1,0:T(8,128)(2,1)S(1)}, bf16[256,256]{1,0:T(8,128)(2,1)}, u32[]{:S(2)}) %copy-start.4) | copy-done | bytes 131096
  6.0 0.0 copy-start.5
  6.0 0.9 %copy-done.5 = f32[80,256]{1,0:T(8,128)S(1)} copy-done((f32[80,256]{1,0:T(8,128)S(1)}, f32[80,256]{1,0:T(8,128)}, u32[]{:S(2)}) %copy-start.5) | copy-done | bytes 81944
  6.9 0.0 copy-start.6
  6.9 0.8 %copy-done.6 = bf16[160,64]{1,0:T(8,128)(2,1)S(1)} copy-done((bf16[160,64]{1,0:T(8,128)(2,1)S(1)}, bf16[160,64]{1,0:T(8,128)(2,1)}, u32[]{:S(2)}) %copy-start.6) | copy-done | bytes 20504
  7.7 0.0 copy-start.7
  7.7 0.8 %copy-done.7 = bf16[64,160]{1,0:T(8,128)(2,1)S(1)} copy-done((bf16[64,160]{1,0:T(8,128)(2,1)S(1)}, bf16[64,160]{1,0:T(8,128)(2,1)}, u32[]{:S(2)}) %copy-start.7) | copy-done | bytes 20504
  8.4 54.2 %shard_map.122 = (bf16[128,1024]{1,0:T(8,128)(2,1)S(1)}, f32[8,128]{1,0:T(8,128)S(1)}) custom-call(bf16[128,1024]{1,0:T(8,128)(2,1)S(1)} %copy-done, bf16[128,1024]{1,0:T(8,128)(2,1)S(1)} %copy-done.1, bf16[128,1024]{1,0:T(8,128)(2,1)S(1)} %copy-done.2, bf16[8,128]{1,0:T(8,128)(2,1)S(1)} %bitcast.5, s32[8,128]{1,0:T(8,128)S(1)} %bitcast.4, ...), custom_call_target="tpu_custom_call" | custom-call | tf_op jit(solution)/shard_map/pallas_call | solution.py:220
  62.7 0.5 fusion
  63.2 0.7 %copy.14 = bf16[128,1024]{1,0:T(8,128)(2,1)} copy(bf16[128,1024]{1,0:T(8,128)(2,1)S(1)} %get-tuple-element.8) | data formatting | bytes 524288
  (1 shorter events, 0.0 us)
Async XLA Ops:
  0.6 0.7 %copy-start.10 = (bf16[128,8]{0,1:T(8,128)(2,1)S(1)}, bf16[128,8]{0,1:T(8,128)(2,1)}, u32[]{:S(2)}) copy-start(bf16[128,8]{0,1:T(8,128)(2,1)} %param.14) | copy-start | bytes 6148
  0.6 0.7 %copy-start.9 = (s32[1024]{0:T(1024)S(1)}, s32[1024]{0:T(1024)}, u32[]{:S(2)}) copy-start(s32[1024]{0:T(1024)} %gid.1) | copy-start | bytes 12292
  0.7 0.7 %copy-start.8 = (s32[128,8]{0,1:T(8,128)S(1)}, s32[128,8]{0,1:T(8,128)}, u32[]{:S(2)}) copy-start(s32[128,8]{0,1:T(8,128)} %param.15) | copy-start | bytes 12292
  1.4 0.9 %copy-start = (bf16[128,1024]{1,0:T(8,128)(2,1)S(1)}, bf16[128,1024]{1,0:T(8,128)(2,1)}, u32[]{:S(2)}) copy-start(bf16[128,1024]{1,0:T(8,128)(2,1)} %signal.1) | copy-start | bytes 786436
  2.3 0.9 %copy-start.1 = (bf16[128,1024]{1,0:T(8,128)(2,1)S(1)}, bf16[128,1024]{1,0:T(8,128)(2,1)}, u32[]{:S(2)}) copy-start(bf16[128,1024]{1,0:T(8,128)(2,1)} %gate.1) | copy-start | bytes 786436
  3.3 0.9 %copy-start.2 = (bf16[128,1024]{1,0:T(8,128)(2,1)S(1)}, bf16[128,1024]{1,0:T(8,128)(2,1)}, u32[]{:S(2)}) copy-start(bf16[128,1024]{1,0:T(8,128)(2,1)} %curvature.1) | copy-start | bytes 786436
  4.2 0.9 %copy-start.3 = (bf16[256,256]{1,0:T(8,128)(2,1)S(1)}, bf16[256,256]{1,0:T(8,128)(2,1)}, u32[]{:S(2)}) copy-start(bf16[256,256]{1,0:T(8,128)(2,1)} %constant.23.clone.ahead) | copy-start | bytes 393220
  5.1 0.9 %copy-start.4 = (bf16[256,256]{1,0:T(8,128)(2,1)S(1)}, bf16[256,256]{1,0:T(8,128)(2,1)}, u32[]{:S(2)}) copy-start(bf16[256,256]{1,0:T(8,128)(2,1)} %constant.24.clone.back) | copy-start | bytes 393220
  6.0 0.9 %copy-start.5 = (f32[80,256]{1,0:T(8,128)S(1)}, f32[80,256]{1,0:T(8,128)}, u32[]{:S(2)}) copy-start(f32[80,256]{1,0:T(8,128)} %constant.22.clone.turn) | copy-start | bytes 245764
  6.9 0.8 %copy-start.6 = (bf16[160,64]{1,0:T(8,128)(2,1)S(1)}, bf16[160,64]{1,0:T(8,128)(2,1)}, u32[]{:S(2)}) copy-start(bf16[160,64]{1,0:T(8,128)(2,1)} %constant.20.clone.enter) | copy-start | bytes 61444
  7.7 0.8 %copy-start.7 = (bf16[64,160]{1,0:T(8,128)(2,1)S(1)}, bf16[64,160]{1,0:T(8,128)(2,1)}, u32[]{:S(2)}) copy-start(bf16[64,160]{1,0:T(8,128)(2,1)} %constant.21.clone.leave) | copy-start | bytes 61444

commit v2 on v1

v2 whole, which is shorter than its diff:
```python
import math

import jax
import jax.numpy as jnp
import numpy as np
from jax import lax
from jax.experimental import pallas as pl
from jax.experimental.pallas import tpu as pltpu
from jax.sharding import PartitionSpec as P

SPAN = 128
HALF = 64
KEPT = 80
BF16 = jnp.bfloat16
F32 = jnp.float32
MESH = pl.DeviceIdType.MESH
DEPTH = 8
CORES = 2


def tables():
    total = SPAN * SPAN
    k2 = np.arange(KEPT)
    live = (k2 <= SPAN // 2).astype(np.float64)
    n1 = np.arange(HALF)
    outer = 2 * np.pi * (np.outer(k2, n1) % SPAN) / SPAN
    enter = np.concatenate([np.cos(outer) * live[:, None], -np.sin(outer) * live[:, None]])
    weight = live * np.where((k2 == 0) | (k2 == SPAN // 2), 1.0, 2.0)
    leave = np.concatenate([(np.cos(outer) * weight[:, None]).T, (-np.sin(outer) * weight[:, None]).T], axis=1)
    fine = np.arange(SPAN)
    twist = 2 * np.pi * np.outer(k2, fine) / total
    turn = np.concatenate([np.cos(twist), np.sin(twist)], axis=1)
    inner = 2 * np.pi * (np.outer(fine, fine) % SPAN) / SPAN
    cos, sin = np.cos(inner), np.sin(inner)
    ahead = np.block([[cos, -sin], [sin, cos]])
    back = np.block([[cos, sin], [-sin, cos]])
    cast = lambda a: a.astype(np.float32).astype(BF16)
    return cast(enter), cast(leave), turn.astype(np.float32), cast(ahead), cast(back)


def dot(a, b):
    return jnp.dot(a, b, preferred_element_type=F32)


def spread_columns(src, width, wide, cols):
    wide[...] = src[...].astype(F32).reshape(HALF * width, SPAN)
    for c in range(width):
        cols[:, c * SPAN : (c + 1) * SPAN] = wide[pl.ds(c, HALF, stride=width), :].astype(BF16)


def forward(cols, enter, turn, ahead, rows, spec):
    width = spec.shape[0]
    tc, ts = turn[:, :SPAN], turn[:, SPAN:]
    for q in range(0, width, 4):
        mixed = dot(enter[...], cols[:, q * SPAN : (q + 4) * SPAN])
        for c in range(4):
            re = mixed[:KEPT, c * SPAN : (c + 1) * SPAN]
            im = mixed[KEPT:, c * SPAN : (c + 1) * SPAN]
            r0 = (q + c) * KEPT
            rows[r0 : r0 + KEPT, :SPAN] = (re * tc + im * ts).astype(BF16)
            rows[r0 : r0 + KEPT, SPAN:] = (im * tc - re * ts).astype(BF16)
    for q in range(0, width, 4):
        spec[q : q + 4] = dot(rows[q * KEPT : (q + 4) * KEPT, :], ahead[...]).reshape(4, KEPT, 2 * SPAN)


def untwist(block, tc, ts):
    re, im = block[:, :SPAN], block[:, SPAN:]
    return jnp.concatenate([re * tc - im * ts, im * tc + re * ts], axis=0).astype(BF16)


def tiles_of(block):
    return block.astype(F32).T.astype(BF16)


def body(signal_hbm, gate_hbm, curvature_hbm, filters_hbm, probe_hbm, gid_hbm,
         enter_hbm, leave_hbm, regroup_hbm, turn_hbm, ahead_hbm, back_hbm, gated, curved,
         signal, gate, curvature, filters, probe, gid, enter, leave, regroup, turn, ahead, back,
         sig_out, sig_in, tap_in, mix_out, mix_in, prim_out, home, part_out, part_in, sum_out, sum_in,
         wide, tang, cols, rows, sig_spec, tap_spec, back_spec, group_spec, send, recv, load):
    me = lax.axis_index("seq")
    lane = lax.axis_index("chan")
    peers = lax.axis_size("seq")
    lanes = lax.axis_size("chan")
    near_z, near_x = me // CORES % DEPTH, me // (CORES * DEPTH)
    core = me % CORES
    across = peers // (CORES * DEPTH)
    column = across * CORES
    width = sig_in.shape[1]
    chans = width * peers
    groups = filters.shape[0]
    total = SPAN * SPAN
    probe_scale = 1.0 / math.sqrt(HALF * SPAN)

    def seq_of(x, z, half):
        return (x * DEPTH + z) * CORES + half

    loads = [
        pltpu.make_async_copy(src, dst, load.at[i])
        for i, (src, dst) in enumerate([
            (signal_hbm, signal), (filters_hbm, filters), (probe_hbm, probe), (gate_hbm, gate),
            (curvature_hbm, curvature), (enter_hbm, enter), (turn_hbm, turn), (ahead_hbm, ahead),
            (back_hbm, back), (leave_hbm, leave), (regroup_hbm, regroup), (gid_hbm, gid),
        ])
    ]
    for copy in loads:
        copy.start()

    barrier = pltpu.get_barrier_semaphore()

    @pl.loop(1, peers)
    def _(k):
        pl.semaphore_signal(barrier, inc=1, device_id={"seq": lax.rem(me + k, peers)}, device_id_type=MESH)

    def mate(k):
        x = lax.rem(near_x + k // CORES, across)
        return seq_of(x, near_z, lax.rem(core + k, CORES))

    @pl.loop(column, column * lanes)
    def _(k):
        to = {"seq": mate(k % column), "chan": lax.rem(lane + k // column, lanes)}
        pl.semaphore_signal(barrier, inc=1, device_id=to, device_id_type=MESH)

    per = SPAN // width
    loads[0].wait()
    for b in range(chans // SPAN):
        sig_out[b * per : (b + 1) * per] = tiles_of(signal[:, b * SPAN : (b + 1) * SPAN]).reshape(per, width, SPAN)
    sig_in[me] = sig_out[me]
    loads[1].wait()
    loads[2].wait()
    signs = 2.0 * probe[...].astype(F32) - 1.0
    tap_in[near_x, near_z, core] = jnp.concatenate([filters[...].astype(F32), signs], axis=0).astype(BF16)
    loads[3].wait()
    loads[4].wait()
    for b in range(chans // SPAN):
        g32 = gate[:, b * SPAN : (b + 1) * SPAN].astype(F32)
        mixed = g32 * g32 * curvature[:, b * SPAN : (b + 1) * SPAN].astype(F32)
        mix_out[b * per : (b + 1) * per] = tiles_of(mixed).reshape(per, width, SPAN)
    mix_in[me] = mix_out[me]
    pl.semaphore_wait(barrier, peers - 1 + column * (lanes - 1))

    def put(slot, src, dst, to):
        return pltpu.make_async_remote_copy(
            src_ref=src, dst_ref=dst, send_sem=send.at[slot], recv_sem=recv.at[slot],
            device_id=to, device_id_type=MESH,
        )

    def scatter(slot, out, into):
        @pl.loop(1, peers)
        def _(k):
            to = lax.rem(me + k, peers)
            put(slot, out.at[to], into.at[me], {"seq": to}).start()

    def lot(slot, ref, count):
        part = ref.at[pl.ds(0, count)]
        return put(slot, part, part, {"seq": lax.rem(me + 1, peers)})

    own_tap = tap_in.at[near_x, near_z, core]

    @pl.loop(1, DEPTH)
    def _(k):
        put(0, own_tap, own_tap, {"seq": seq_of(near_x, lax.rem(near_z + k, DEPTH), core)}).start()

    scatter(2, sig_out, sig_in)
    lot(0, sig_in, DEPTH - 1).wait_recv()
    own_line = tap_in.at[near_x, :, core]

    @pl.loop(1, column)
    def _(k):
        put(1, own_line, own_line, {"seq": mate(k)}).start()

    scatter(3, mix_out, mix_in)
    for copy in loads[5:]:
        copy.wait()
    tc, ts = turn[:, :SPAN], turn[:, SPAN:]

    lot(1, sig_in, DEPTH * (column - 1)).wait_recv()
    spread_columns(tap_in, width, wide, cols)
    forward(cols, enter, turn, ahead, rows, tap_spec)
    lot(2, sig_in, peers - 1).wait_recv()
    spread_columns(sig_in, width, wide, cols)
    forward(cols, enter, turn, ahead, rows, sig_spec)
    for c in range(width):
        g = gid[me * width + c]
        sr, si = sig_spec[c, :, :SPAN], sig_spec[c, :, SPAN:]
        for kind in range(2):
            taps = tap_spec[g + kind * groups]
            fr, fi = taps[:, :SPAN], taps[:, SPAN:]
            r0 = (2 * c + kind) * KEPT
            rows[r0 : r0 + KEPT, :SPAN] = (sr * fr - si * fi).astype(BF16)
            rows[r0 : r0 + KEPT, SPAN:] = (sr * fi + si * fr).astype(BF16)
        inner = dot(rows[2 * c * KEPT : 2 * (c + 1) * KEPT, :], back[...])
        both = jnp.concatenate([untwist(inner[:KEPT], tc, ts), untwist(inner[KEPT:], tc, ts)], axis=1)
        timed = dot(leave[...], both)
        wide[pl.ds(c, HALF, stride=width), :] = timed[:, :SPAN] * (1.0 / total)
        tang[c] = timed[:, SPAN:] * (probe_scale / total)
    prim_out[...] = wide[...].astype(BF16).reshape(prim_out.shape)
    home[me] = prim_out[me]
    scatter(4, prim_out, home)

    lot(3, mix_in, peers - 1).wait_recv()
    wide[...] = mix_in[...].astype(F32).reshape(HALF * width, SPAN)
    for c in range(width):
        tangent = tang[c].astype(BF16).astype(F32)
        cols[:, c * SPAN : (c + 1) * SPAN] = (tangent * wide[pl.ds(c, HALF, stride=width), :]).astype(BF16)
    forward(cols, enter, turn, ahead, rows, back_spec)
    for c in range(width):
        sr, si = sig_spec[c, :, :SPAN], sig_spec[c, :, SPAN:]
        br, bi = back_spec[c, :, :SPAN], back_spec[c, :, SPAN:]
        back_spec[c] = jnp.concatenate([sr * br + si * bi, sr * bi - si * br], axis=1)
    for g in range(groups):
        acc = jnp.zeros((KEPT, 2 * SPAN), F32)
        for c in range(width):
            acc = acc + jnp.where(gid[me * width + c] == g, 1.0, 0.0).astype(F32) * back_spec[c]
        group_spec[g * KEPT : (g + 1) * KEPT, :] = acc.astype(BF16)
    share = groups // lanes
    for g in range(0, groups, share):
        inner = dot(group_spec[g * KEPT : (g + share) * KEPT, :], back[...])
        both = jnp.concatenate([untwist(inner[i * KEPT : (i + 1) * KEPT], tc, ts) for i in range(share)], axis=1)
        timed = dot(regroup[...], both)
        for i in range(share):
            block = timed[:, i * SPAN : (i + 1) * SPAN].reshape(column, DEPTH, SPAN)
            part_out[g // share * column : (g // share + 1) * column, i * DEPTH : (i + 1) * DEPTH] = block
    mine = lane * column + near_x * CORES + core
    part_in[mine] = part_out[mine]

    @pl.loop(1, column * lanes)
    def _(k):
        seq, chan = mate(k % column), lax.rem(lane + k // column, lanes)
        slot = chan * column + (seq // (CORES * DEPTH)) * CORES + seq % CORES
        put(5, part_out.at[slot], part_in.at[mine], {"seq": seq, "chan": chan}).start()

    lot(4, home, peers - 1).wait_recv()
    for b in range(chans // SPAN):
        block = home[b * per : (b + 1) * per].reshape(SPAN, SPAN)
        span = slice(b * SPAN, (b + 1) * SPAN)
        gated[:, span] = (gate[:, span].astype(F32) * block.astype(F32).T).astype(BF16)

    lot(5, part_in, column * lanes - 1).wait_recv()
    summed = jnp.sum(part_in[...], axis=0)
    sum_out[...] = jnp.zeros_like(sum_out)
    for i in range(share):
        sum_out[pl.ds(i, DEPTH, stride=8), :] = summed[i * DEPTH : (i + 1) * DEPTH]
    sum_in[near_z] = sum_out[pl.ds(pl.multiple_of(near_z * 8, 8), 8), :]

    @pl.loop(1, DEPTH)
    def _(k):
        z = lax.rem(near_z + k, DEPTH)
        src = sum_out.at[pl.ds(pl.multiple_of(z * 8, 8), 8)]
        put(6, src, sum_in.at[near_z], {"seq": seq_of(near_x, z, core)}).start()

    lot(0, sig_out, DEPTH - 1).wait_send()
    lot(1, sig_out, DEPTH * (column - 1)).wait_send()
    lot(2, sig_out, peers - 1).wait_send()
    lot(3, mix_out, peers - 1).wait_send()
    lot(4, prim_out, peers - 1).wait_send()
    lot(5, part_out, column * lanes - 1).wait_send()
    lot(6, sum_in, DEPTH - 1).wait()
    scale = 1.0 / (math.sqrt(HALF * SPAN * chans * lanes / groups) * total)
    curved[...] = (jnp.sum(sum_in[...], axis=0)[:share] * scale).astype(BF16)


def local(signal, gate, curvature, filters, probe, group_ids):
    peers, lanes = lax.axis_size("seq"), lax.axis_size("chan")
    seq_rows, chans = signal.shape
    groups = filters.shape[1]
    width = chans // peers
    across = peers // (CORES * DEPTH)
    column = across * CORES
    vmem = pl.BlockSpec(memory_space=pltpu.VMEM)
    hbm = pl.BlockSpec(memory_space=pltpu.HBM)
    tile = pltpu.VMEM((peers, width, seq_rows), BF16)
    inputs = [signal, gate, curvature, filters.T, probe.T, group_ids]
    enter, leave, turn, ahead, back = tables()
    order = np.arange(peers).reshape(across, DEPTH, CORES).transpose(0, 2, 1).reshape(-1)
    inputs += [jnp.asarray(t) for t in (enter, leave, leave[order], turn, ahead, back)]
    output_mix, curved = pl.pallas_call(
        body,
        out_shape=(
            jax.ShapeDtypeStruct((seq_rows, chans), BF16),
            jax.ShapeDtypeStruct((groups // lanes, seq_rows), BF16),
        ),
        in_specs=[hbm] * len(inputs),
        out_specs=(vmem, vmem),
        scratch_shapes=[
            (pltpu.SMEM if a is group_ids else pltpu.VMEM)(a.shape, a.dtype) for a in inputs
        ] + [
            tile,
            tile,
            pltpu.VMEM((across, DEPTH, CORES, width, seq_rows), BF16),
            tile,
            tile,
            tile,
            tile,
            pltpu.VMEM((column * lanes, groups // lanes * DEPTH, seq_rows), F32),
            pltpu.VMEM((column * lanes, groups // lanes * DEPTH, seq_rows), F32),
            pltpu.VMEM((8 * DEPTH, seq_rows), F32),
            pltpu.VMEM((DEPTH, 8, seq_rows), F32),
            pltpu.VMEM((HALF * width, SPAN), F32),
            pltpu.VMEM((width, HALF, SPAN), F32),
            pltpu.VMEM((HALF, width * SPAN), BF16),
            pltpu.VMEM((2 * width * KEPT, 2 * SPAN), BF16),
            pltpu.VMEM((width, KEPT, 2 * SPAN), F32),
            pltpu.VMEM((2 * groups, KEPT, 2 * SPAN), F32),
            pltpu.VMEM((width, KEPT, 2 * SPAN), F32),
            pltpu.VMEM((groups * KEPT, 2 * SPAN), BF16),
            pltpu.SemaphoreType.DMA((7,)),
            pltpu.SemaphoreType.DMA((7,)),
            pltpu.SemaphoreType.DMA((len(inputs),)),
        ],
        compiler_params=pltpu.CompilerParams(
            collective_id=0, has_side_effects=True, vmem_limit_bytes=67043328
        ),
    )(*inputs)
    return (output_mix, curved.T)


def solution(mesh):
    return jax.shard_map(
        local,
        mesh=mesh,
        in_specs=(
            P("seq", "chan"),
            P("seq", "chan"),
            P("seq", "chan"),
            P("seq", None),
            P("seq", None),
            P("chan"),
        ),
        out_specs=(P("seq", "chan"), P("seq", "chan")),
        check_vma=False,
    )
```

time: 64.3 us -> 47.4 us (0.74)
  Pallas kernels: 54.2 us -> 44.5 us
  local copies, waits for them, and re-layouts: 9 us -> 2.18 us
    pallas_call x1, Pallas kernels: 54.2 us -> 44.5 us  [local(): pl.pallas_call(body, out_shape=(jax.ShapeDtypeStruct((seq_rows, chans), B...]
    unnamed x23 -> x4, local copies, waits for them, and re-layouts: 8.47 us -> 2.18 us
where the time goes in v2:
time: 47.4 us; the launch traced here: 47.3 us
  Pallas kernels  44.5 us (94%)
  local copies, waits for them, and re-layouts  2.18 us (5%)
  between operations  0.65 us (1%)
    pallas_call x1, Pallas kernels, local(): pl.pallas_call(body, out_shape=(jax.ShapeDtypeStruct((seq_rows, chans), B...  44.5 us
    unnamed x4, local copies, waits for them, and re-layouts  2.18 us

profile of v2, /device:TPU:1, one launch (start us, length us, event | category | flops | bytes accessed | tf_op | source)
XLA Modules:
  0.0 47.3 jit_solution(10607924676449314541)
XLA Ops:
  0.6 44.5 %shard_map.131 = (bf16[128,1024]{1,0:T(8,128)(2,1)}, bf16[2,128]{1,0:T(2,128)(2,1)}) custom-call(bf16[128,1024]{1,0:T(8,128)(2,1)} %signal_hbm.1, bf16[128,1024]{1,0:T(8,128)(2,1)} %gate_hbm.1, bf16[128,1024]{1,0:T(8,128)(2,1)} %curvature_hbm.1, bf16[8,128]{1,0:T(8,128)(2,1)} %bitcast.4, s32[8,128]{1,0:T(8,128)} %bitcast.3, s32[1024]{0:T(1024)} %gid_hbm.1, ...), custom_call_target="tpu_custom_call" | custom-call | tf_op jit(solution)/shard_map/pallas_call | solution.py:276
  45.1 0.0 copy-start
  45.1 1.7 %copy.16 = bf16[128,1024]{1,0:T(8,128)(2,1)} copy(bf16[128,1024]{1,0:T(8,128)(2,1)} %get-tuple-element.8) | data formatting | bytes 524288
  46.8 0.0 copy-done
  46.8 0.5 %copy.17 = bf16[128,2]{0,1:T(2,128)(2,1)} copy(bf16[128,2]{0,1:T(2,128)(2,1)S(1)} %bitcast.5) | data formatting | bytes 1024
Async XLA Ops:
  45.1 1.7 %copy-start = (bf16[2,128]{1,0:T(2,128)(2,1)S(1)}, bf16[2,128]{1,0:T(2,128)(2,1)}, u32[]{:S(2)}) copy-start(bf16[2,128]{1,0:T(2,128)(2,1)} %get-tuple-element.5) | copy-start | bytes 1540

commit v3 on v2

--- a/solution.py
+++ b/solution.py
@@ -145,9 +145,14 @@
         )
 
     def scatter(slot, out, into):
-        @pl.loop(1, peers)
+        @pl.loop(0, peers - 1)
         def _(k):
-            to = lax.rem(me + k, peers)
+            rank = k % DEPTH
+            far = DEPTH // 2 - (rank + 1) // 2
+            z = lax.rem(near_z + jnp.where(rank % 2 == 1, far, DEPTH - far), DEPTH)
+            rest = (k // DEPTH + rank + 2 + DEPTH * (column - 1)) % column
+            x = lax.rem(near_x + rest // CORES, across)
+            to = seq_of(x, z, lax.rem(core + rest, CORES))
             put(slot, out.at[to], into.at[me], {"seq": to}).start()
 
     def lot(slot, ref, count):
@@ -217,9 +222,8 @@
         inner = dot(group_spec[g * KEPT : (g + share) * KEPT, :], back[...])
         both = jnp.concatenate([untwist(inner[i * KEPT : (i + 1) * KEPT], tc, ts) for i in range(share)], axis=1)
         timed = dot(regroup[...], both)
-        for i in range(share):
-            block = timed[:, i * SPAN : (i + 1) * SPAN].reshape(column, DEPTH, SPAN)
-            part_out[g // share * column : (g // share + 1) * column, i * DEPTH : (i + 1) * DEPTH] = block
+        parts = [timed[:, i * SPAN : (i + 1) * SPAN].reshape(column, DEPTH, SPAN) for i in range(share)]
+        part_out[g // share * column : (g // share + 1) * column] = jnp.concatenate(parts, axis=1).astype(BF16)
     mine = lane * column + near_x * CORES + core
     part_in[mine] = part_out[mine]
 
@@ -228,25 +232,25 @@
         seq, chan = mate(k % column), lax.rem(lane + k // column, lanes)
         slot = chan * column + (seq // (CORES * DEPTH)) * CORES + seq % CORES
         put(5, part_out.at[slot], part_in.at[mine], {"seq": seq, "chan": chan}).start()
+
+    lot(5, part_in, column * lanes - 1).wait_recv()
+    summed = jnp.sum(part_in[...].astype(F32), axis=0)
+    sum_out[...] = jnp.zeros_like(sum_out)
+    for i in range(share):
+        sum_out[pl.ds(i, DEPTH, stride=8), :] = summed[i * DEPTH : (i + 1) * DEPTH]
+    sum_in[near_z] = sum_out[pl.ds(pl.multiple_of(near_z * 8, 8), 8), :]
+
+    @pl.loop(1, DEPTH)
+    def _(k):
+        z = lax.rem(near_z + k, DEPTH)
+        src = sum_out.at[pl.ds(pl.multiple_of(z * 8, 8), 8)]
+        put(6, src, sum_in.at[near_z], {"seq": seq_of(near_x, z, core)}).start()
 
     lot(4, home, peers - 1).wait_recv()
     for b in range(chans // SPAN):
         block = home[b * per : (b + 1) * per].reshape(SPAN, SPAN)
         span = slice(b * SPAN, (b + 1) * SPAN)
         gated[:, span] = (gate[:, span].astype(F32) * block.astype(F32).T).astype(BF16)
-
-    lot(5, part_in, column * lanes - 1).wait_recv()
-    summed = jnp.sum(part_in[...], axis=0)
-    sum_out[...] = jnp.zeros_like(sum_out)
-    for i in range(share):
-        sum_out[pl.ds(i, DEPTH, stride=8), :] = summed[i * DEPTH : (i + 1) * DEPTH]
-    sum_in[near_z] = sum_out[pl.ds(pl.multiple_of(near_z * 8, 8), 8), :]
-
-    @pl.loop(1, DEPTH)
-    def _(k):
-        z = lax.rem(near_z + k, DEPTH)
-        src = sum_out.at[pl.ds(pl.multiple_of(z * 8, 8), 8)]
-        put(6, src, sum_in.at[near_z], {"seq": seq_of(near_x, z, core)}).start()
 
     lot(0, sig_out, DEPTH - 1).wait_send()
     lot(1, sig_out, DEPTH * (column - 1)).wait_send()
@@ -291,8 +295,8 @@
             tile,
             tile,
             tile,
-            pltpu.VMEM((column * lanes, groups // lanes * DEPTH, seq_rows), F32),
-            pltpu.VMEM((column * lanes, groups // lanes * DEPTH, seq_rows), F32),
+            pltpu.VMEM((column * lanes, groups // lanes * DEPTH, seq_rows), BF16),
+            pltpu.VMEM((column * lanes, groups // lanes * DEPTH, seq_rows), BF16),
             pltpu.VMEM((8 * DEPTH, seq_rows), F32),
             pltpu.VMEM((DEPTH, 8, seq_rows), F32),
             pltpu.VMEM((HALF * width, SPAN), F32),

time: 47.4 us -> 47 us (level)
  no operation moved by 1% of the time
where the time goes in v3:
time: 47 us; the launch traced here: 46.9 us
  Pallas kernels  44.1 us (94%)
  local copies, waits for them, and re-layouts  2.18 us (5%)
  between operations  0.65 us (1%)
    pallas_call x1, Pallas kernels, local(): pl.pallas_call(body, out_shape=(jax.ShapeDtypeStruct((seq_rows, chans), B...  44.1 us
    unnamed x4, local copies, waits for them, and re-layouts  2.18 us

profile of v3, /device:TPU:1, one launch (start us, length us, event | category | flops | bytes accessed | tf_op | source)
XLA Modules:
  0.0 46.9 jit_solution(10639420179620095570)
XLA Ops:
  0.6 44.1 %shard_map.131 = (bf16[128,1024]{1,0:T(8,128)(2,1)}, bf16[2,128]{1,0:T(2,128)(2,1)}) custom-call(bf16[128,1024]{1,0:T(8,128)(2,1)} %signal_hbm.1, bf16[128,1024]{1,0:T(8,128)(2,1)} %gate_hbm.1, bf16[128,1024]{1,0:T(8,128)(2,1)} %curvature_hbm.1, bf16[8,128]{1,0:T(8,128)(2,1)} %bitcast.4, s32[8,128]{1,0:T(8,128)} %bitcast.3, s32[1024]{0:T(1024)} %gid_hbm.1, ...), custom_call_target="tpu_custom_call" | custom-call | tf_op jit(solution)/shard_map/pallas_call | solution.py:280
  44.7 0.0 copy-start
  44.7 1.7 %copy.16 = bf16[128,1024]{1,0:T(8,128)(2,1)} copy(bf16[128,1024]{1,0:T(8,128)(2,1)} %get-tuple-element.8) | data formatting | bytes 524288
  46.4 0.0 copy-done
  46.4 0.5 %copy.17 = bf16[128,2]{0,1:T(2,128)(2,1)} copy(bf16[128,2]{0,1:T(2,128)(2,1)S(1)} %bitcast.5) | data formatting | bytes 1024
Async XLA Ops:
  44.7 1.7 %copy-start = (bf16[2,128]{1,0:T(2,128)(2,1)S(1)}, bf16[2,128]{1,0:T(2,128)(2,1)}, u32[]{:S(2)}) copy-start(bf16[2,128]{1,0:T(2,128)(2,1)} %get-tuple-element.5) | copy-start | bytes 1540

commit v4 on v3

--- a/solution.py
+++ b/solution.py
@@ -16,6 +16,7 @@
 MESH = pl.DeviceIdType.MESH
 DEPTH = 8
 CORES = 2
+VMEM_LIMIT = 16 << 20
 
 
 def tables():
@@ -129,13 +130,6 @@
     loads[2].wait()
     signs = 2.0 * probe[...].astype(F32) - 1.0
     tap_in[near_x, near_z, core] = jnp.concatenate([filters[...].astype(F32), signs], axis=0).astype(BF16)
-    loads[3].wait()
-    loads[4].wait()
-    for b in range(chans // SPAN):
-        g32 = gate[:, b * SPAN : (b + 1) * SPAN].astype(F32)
-        mixed = g32 * g32 * curvature[:, b * SPAN : (b + 1) * SPAN].astype(F32)
-        mix_out[b * per : (b + 1) * per] = tiles_of(mixed).reshape(per, width, SPAN)
-    mix_in[me] = mix_out[me]
     pl.semaphore_wait(barrier, peers - 1 + column * (lanes - 1))
 
     def put(slot, src, dst, to):
@@ -166,6 +160,13 @@
         put(0, own_tap, own_tap, {"seq": seq_of(near_x, lax.rem(near_z + k, DEPTH), core)}).start()
 
     scatter(2, sig_out, sig_in)
+    loads[3].wait()
+    loads[4].wait()
+    for b in range(chans // SPAN):
+        g32 = gate[:, b * SPAN : (b + 1) * SPAN].astype(F32)
+        mixed = g32 * g32 * curvature[:, b * SPAN : (b + 1) * SPAN].astype(F32)
+        mix_out[b * per : (b + 1) * per] = tiles_of(mixed).reshape(per, width, SPAN)
+    mix_in[me] = mix_out[me]
     lot(0, sig_in, DEPTH - 1).wait_recv()
     own_line = tap_in.at[near_x, :, core]
 
@@ -312,9 +313,9 @@
             pltpu.SemaphoreType.DMA((len(inputs),)),
         ],
         compiler_params=pltpu.CompilerParams(
-            collective_id=0, has_side_effects=True, vmem_limit_bytes=67043328
+            collective_id=0, has_side_effects=True, vmem_limit_bytes=VMEM_LIMIT
         ),
-    )(*inputs)
+    )(*[pltpu.with_memory_space_constraint(a, pltpu.HBM) for a in inputs])
     return (output_mix, curved.T)
 
 

time: 47 us -> 45.3 us (0.964)
  local copies, waits for them, and re-layouts: 2.18 us -> 1.22 us
  Pallas kernels: 44.1 us -> 43.4 us
    unnamed x4 -> x2, local copies, waits for them, and re-layouts: 2.18 us -> 1.22 us
    pallas_call x1, Pallas kernels: 44.1 us -> 43.4 us  [local(): pl.pallas_call(body, out_shape=(jax.ShapeDtypeStruct((seq_rows, chans), B...]
where the time goes in v4:
time: 45.3 us; the launch traced here: 45.2 us
  Pallas kernels  43.4 us (96%)
  local copies, waits for them, and re-layouts  1.22 us (3%)
  between operations  0.64 us (1%)
    pallas_call x1, Pallas kernels, local(): pl.pallas_call(body, out_shape=(jax.ShapeDtypeStruct((seq_rows, chans), B...  43.4 us
    unnamed x2, local copies, waits for them, and re-layouts  1.22 us

profile of v4, /device:TPU:1, one launch (start us, length us, event | category | flops | bytes accessed | tf_op | source)
XLA Modules:
  0.0 45.2 jit_solution(10113814350754129382)
XLA Ops:
  0.6 43.4 %shard_map.131 = (bf16[128,1024]{1,0:T(8,128)(2,1)S(1)}, bf16[2,128]{1,0:T(2,128)(2,1)S(1)}) custom-call(bf16[128,1024]{1,0:T(8,128)(2,1)} %signal_hbm.1, bf16[128,1024]{1,0:T(8,128)(2,1)} %gate_hbm.1, bf16[128,1024]{1,0:T(8,128)(2,1)} %curvature_hbm.1, bf16[8,128]{1,0:T(8,128)(2,1)} %bitcast.5, s32[8,128]{1,0:T(8,128)} %bitcast.4, s32[1024]{0:T(1024)} %gid_hbm.1, ...), custom_call_target="tpu_custom_call" | custom-call | tf_op jit(solution)/shard_map/pallas_call | solution.py:281
  44.0 0.7 %copy.16 = bf16[128,1024]{1,0:T(8,128)(2,1)} copy(bf16[128,1024]{1,0:T(8,128)(2,1)S(1)} %get-tuple-element.8) | data formatting | bytes 524288
  44.7 0.5 %copy.17 = bf16[128,2]{0,1:T(2,128)(2,1)} copy(bf16[128,2]{0,1:T(2,128)(2,1)S(1)} %bitcast.3) | data formatting | bytes 1024
